TPU v7x, 256 devices: a whole 4x4x8 slice. The times are simulated.
256 devices in a mesh: seq: 64 (over y, z, core), tp: 4 (over x).
Axes of the slice: x: 4, y: 4, z: 8, core: 2. Of those that a mesh axis runs over, the one named last changes fastest.
Arguments:
- stream: bfloat16 [8192, 2048], P('seq'), may hold values from -256 to 256
- lengths: int32 [6], replicated, may hold values from 1 to 7168, 8192 in all
- q_weight: bfloat16 [2048, 1536], P(None, 'tp'), may hold values from -0.125 to 0.125
- kv_down: bfloat16 [2048, 576], replicated, may hold values from -0.125 to 0.125
- latent_gain: float32 [512], replicated, may hold values from 0.1 to 1.9
- kv_up: bfloat16 [8, 512, 256], P('tp'), may hold values from -0.25 to 0.25
- out_weight: bfloat16 [1024, 2048], P('tp'), may hold values from -0.1875 to 0.1875
- moe_gain: float32 [2048], replicated, may hold values from 0.1 to 1.9
- routes: int32 [8192, 6], P('seq'), may hold values from 0 to 63, all different within a row; in each aligned block of 128 rows (0 to 127, 128 to 255, ...) at most 24 rows name the same one
- route_weight: float32 [8192, 6], P('seq'), may hold values from 0.05 to 0.5
- expert_gate: bfloat16 [64, 2048, 1408], P('seq', None, 'tp'), may hold values from -0.125 to 0.125
- expert_up: bfloat16 [64, 2048, 1408], P('seq', None, 'tp'), may hold values from -0.125 to 0.125
- expert_down: bfloat16 [64, 1408, 2048], P('seq', 'tp'), may hold values from -0.15625 to 0.15625
Outputs:
- layer_out: bfloat16 [8192, 2048], P('seq')
- latent_cache: bfloat16 [8192, 576], P('seq')
Inputs may be any that keep to these rules, and one draw needn't show every extreme that they name: 6 lengths summing to 8192, the longest exactly 7168. In each aligned block of 128 rows no expert is named by more than 24 routes, a bound that some block reaches.
All inputs are finite; a program needn't handle non-finite values.
Results may differ from a plain program's by a relative error of at most 0.0075.
Values may be sent and summed in bfloat16 or wider, within the bound.
A program may use at most 128 MiB of HBM per device.

v0:
```python
import jax
import jax.numpy as jnp
from jax import lax
from jax.sharding import PartitionSpec as P

D = 2048
NOPE = 128
ROPE = 64
LATENT = 512
VDIM = 128
THETA = 50000.0


def place(token_index, lengths):
    prompt_ends = jnp.cumsum(lengths)
    before = (prompt_ends[None, :] <= token_index[:, None]).astype(jnp.int32)
    segment = jnp.sum(before, axis=1)
    prompt_start = jnp.sum(before * lengths[None, :], axis=1)
    return (segment, token_index - prompt_start)


def angles(position):
    half_rope = ROPE // 2
    frequency = THETA ** (-2.0 * jnp.arange(half_rope, dtype=jnp.float32) / ROPE)
    angle_table = position.astype(jnp.float32)[:, None] * frequency[None, :]
    return (jnp.cos(angle_table), jnp.sin(angle_table))


def rotate(values, cos_table, sin_table):
    half_rope = ROPE // 2
    first_half = values[..., :half_rope]
    second = values[..., half_rope:]
    return jnp.concatenate(
        [first_half * cos_table - second * sin_table, first_half * sin_table + second * cos_table],
        axis=-1,
    )


def on_device(
    stream,
    lengths,
    q_weight,
    kv_down,
    latent_gain,
    kv_up,
    out_weight,
    moe_gain,
    routes,
    route_weight,
    expert_gate,
    expert_up,
    expert_down,
):
    tok_count = stream.shape[0]
    head_count = kv_up.shape[0]
    first_row = lax.axis_index("seq") * tok_count
    token_index = first_row + jnp.arange(tok_count, dtype=jnp.int32)
    segment, position = place(token_index, lengths)
    cos_table, sin_table = angles(position)
    kv_proj = jnp.dot(stream, kv_down, preferred_element_type=jnp.float32)
    compressed = kv_proj[:, :LATENT]
    factor = lax.rsqrt(jnp.mean(compressed * compressed, axis=1, keepdims=True) + 1e-06)
    latent = jnp.concatenate(
        [
            compressed * factor * latent_gain[None, :],
            rotate(kv_proj[:, LATENT:], cos_table, sin_table),
        ],
        axis=1,
    ).astype(jnp.bfloat16)
    q_proj = jnp.dot(stream, q_weight, preferred_element_type=jnp.float32).astype(jnp.bfloat16)
    q_proj = q_proj.reshape(tok_count, head_count, NOPE + ROPE)
    absorbed = jnp.einsum(
        "thj,hcj->thc", q_proj[:, :, :NOPE], kv_up[:, :, :NOPE], preferred_element_type=jnp.float32
    )
    rotated = rotate(
        q_proj[:, :, NOPE:].astype(jnp.float32), cos_table[:, None, :], sin_table[:, None, :]
    )
    softmax_scale = (NOPE + ROPE) ** (-0.5)
    queries = (jnp.concatenate([absorbed, rotated], axis=2) * softmax_scale).astype(jnp.bfloat16)
    queries = queries.reshape(tok_count * head_count, LATENT + ROPE)
    row_segment = jnp.repeat(segment, head_count)
    row_index = jnp.repeat(token_index, head_count)
    row_total = tok_count * head_count
    shard_rows = lax.all_gather(latent, "seq", axis=0, tiled=True)
    key_count = shard_rows.shape[0]
    key_index = jnp.arange(key_count, dtype=jnp.int32)
    key_segment, unused = place(key_index, lengths)
    allowed = (row_segment[:, None] == key_segment[None, :]) & (
        key_index[None, :] <= row_index[:, None]
    )
    running_max = jnp.full((row_total,), -1e30, jnp.float32)
    scores = jnp.einsum("ra,ka->rk", queries, shard_rows, preferred_element_type=jnp.float32)
    block_peak = jnp.max(jnp.where(allowed, scores, -jnp.inf), axis=1)
    new_peak = jnp.maximum(running_max, block_peak)
    weights = jnp.where(allowed, jnp.exp(scores - new_peak[:, None]), 0.0)
    running_sum = jnp.sum(weights, axis=1)
    context_sum = jnp.dot(
        weights.astype(jnp.bfloat16), shard_rows[:, :LATENT], preferred_element_type=jnp.float32
    )
    running_max, running_sum, context_sum = (new_peak, running_sum, context_sum)
    context = (context_sum / running_sum[:, None]).reshape(tok_count, head_count, LATENT)
    heads_out = jnp.einsum(
        "thc,hcv->thv",
        context,
        kv_up[:, :, NOPE:].astype(jnp.float32),
        precision=lax.Precision.HIGHEST,
    )
    heads_out = heads_out.astype(jnp.bfloat16).reshape(tok_count, head_count * VDIM)
    partial_attention = jnp.dot(heads_out, out_weight, preferred_element_type=jnp.float32)
    tp_count = lax.axis_size("tp")
    col_width = D // tp_count
    col_start = lax.axis_index("tp") * col_width
    attention_pieces = partial_attention.astype(jnp.bfloat16).reshape(
        tok_count, tp_count, col_width
    )
    attention_pieces = lax.all_to_all(
        attention_pieces.transpose(1, 0, 2), "tp", split_axis=0, concat_axis=0, tiled=True
    )
    attention_part = jnp.sum(attention_pieces.astype(jnp.float32), axis=0)
    stream_part = lax.dynamic_slice_in_dim(stream, col_start, col_width, 1)
    hidden = stream_part.astype(jnp.float32) + attention_part
    normed = hidden.astype(jnp.bfloat16)
    experts = lax.axis_size("seq")
    top_k = routes.shape[1]
    capacity = min(tok_count, max(2, 2 * tok_count * top_k // experts))
    flat_routes = routes.reshape(-1)
    onehot = (flat_routes[:, None] == jnp.arange(experts, dtype=jnp.int32)[None, :]).astype(
        jnp.int32
    )
    slot_rank = jnp.sum((jnp.cumsum(onehot, axis=0) - onehot) * onehot, axis=1)
    slot_index = flat_routes * capacity + slot_rank
    slot_table = (
        slot_index[:, None] == jnp.arange(experts * capacity, dtype=jnp.int32)[None, :]
    ).astype(jnp.bfloat16)
    placing = jnp.sum(slot_table.reshape(tok_count, top_k, experts * capacity), axis=1)
    outgoing = jnp.einsum("ts,td->sd", placing, normed, preferred_element_type=jnp.float32).astype(
        jnp.bfloat16
    )
    outgoing = outgoing.reshape(experts, capacity, col_width)
    chunk_count = 2
    chunk_slots = capacity // chunk_count
    returned_chunks = []
    for chunk in range(chunk_count):
        sending = outgoing[:, chunk * chunk_slots : (chunk + 1) * chunk_slots]
        received = lax.all_to_all(sending, "seq", split_axis=0, concat_axis=0, tiled=True)
        sources, slot_count, _ = received.shape
        flat_part = received.reshape(sources * slot_count, col_width)
        flat_rows = lax.all_gather(flat_part, "tp", axis=1, tiled=True).astype(jnp.float32)
        flat_rows = (
            flat_rows
            * lax.rsqrt(jnp.mean(flat_rows * flat_rows, axis=1, keepdims=True) + 1e-06)
            * moe_gain[None, :]
        ).astype(jnp.bfloat16)
        gate_act = jnp.dot(flat_rows, expert_gate[0], preferred_element_type=jnp.float32)
        up_act = jnp.dot(flat_rows, expert_up[0], preferred_element_type=jnp.float32)
        hidden_units = (jax.nn.silu(gate_act) * up_act).astype(jnp.bfloat16)
        expert_out = jnp.dot(
            hidden_units, expert_down[0], preferred_element_type=jnp.float32
        ).astype(jnp.bfloat16)
        expert_sum = lax.psum_scatter(expert_out, "tp", scatter_dimension=1, tiled=True)
        expert_sum = expert_sum.reshape(sources, slot_count, col_width)
        returned_chunks.append(
            lax.all_to_all(expert_sum, "seq", split_axis=0, concat_axis=0, tiled=True)
        )
    returned = jnp.concatenate(returned_chunks, axis=1)
    gathered = returned.reshape(experts * capacity, col_width)[slot_index].reshape(
        tok_count, top_k, col_width
    )
    moe = jnp.zeros((tok_count, col_width), jnp.float32)
    for route_slot in range(top_k):
        moe = moe + route_weight[:, route_slot][:, None] * gathered[:, route_slot].astype(
            jnp.float32
        )
    layer_part = (hidden + moe).astype(jnp.bfloat16)
    repeated_part = jnp.broadcast_to(layer_part[None], (tp_count,) + layer_part.shape)
    layer_pieces = lax.all_to_all(repeated_part, "tp", split_axis=0, concat_axis=0, tiled=True)
    layer_out = layer_pieces.transpose(1, 0, 2).reshape(tok_count, D)
    return (layer_out, latent)


def solution(mesh):
    return jax.shard_map(
        on_device,
        mesh=mesh,
        in_specs=(
            P("seq", None),
            P(),
            P(None, "tp"),
            P(),
            P(),
            P("tp", None, None),
            P("tp", None),
            P(),
            P("seq", None),
            P("seq", None),
            P("seq", None, "tp"),
            P("seq", None, "tp"),
            P("seq", "tp", None),
        ),
        out_specs=(P("seq", None), P("seq", None)),
        check_vma=False,
    )
```

profile of v0, /device:TPU:1, one launch (start us, length us, event | category | flops | bytes accessed | tf_op | source)
XLA Modules:
  0.0 411.8 jit_solution(14239379274214092569)
XLA Ops:
  7.3 1.0 reduce-window.18
  8.3 0.7 fusion.82
  9.1 1.9 fusion.94
  11.3 0.7 pad_maximum_fusion.1
  12.4 1.8 convolution_convert_fusion.4
  15.4 0.4 copy.95
  15.8 0.4 concatenate.17
  16.2 1.8 reduce-window.19
  18.0 0.3 slice_reduce_fusion
  18.8 84.7 %all-gather.4.cloned.1.call-done = bf16[8192,576]{0,1:T(8,128)(2,1)} async-done(((bf16[128,576]{0,1:T(8,128)(2,1)}), bf16[8192,576]{0,1:T(8,128)(2,1)}) %all-gather.4.cloned.1.call-update) | async-done | bytes 9437200 | tf_op jit(solution)/shard_map/all_gather | solution.py:84
  103.5 6.8 %select_reduce_fusion = (f32[256]{0:T(256)S(1)}, f32[256,8192]{1,0:T(8,128)S(1)}) fusion(s32[256]{0:T(256)S(1)} %le.48, s32[8192]{0:T(1024)S(1)} %convert_reduce_fusion.1, s32[256]{0:T(256)S(1)} %eq.54, bf16[8192,576]{0,1:T(8,128)(2,1)} %all-gather.4.cloned.1.call-done, f32[256,32]{1,0:T(8,128)S(1)} %bitcast.130, f32[256,32]{1,0:T(8,128)S(1)} %bitcast.129, ...), kind=kOutput, calls=%fused_computation.4 | convolution fusion | flops 2426994432 | bytes 18451456 | tf_op jit(solution)/shard_map/ra,ka->rk/dot_general | solution.py:92
  110.3 2.8 fusion.9
  113.1 6.3 %fusion.41 = f32[256,512]{1,0:T(8,128)S(1)} fusion(bf16[8192,576]{0,1:T(8,128)(2,1)} %all-gather.4.cloned.1.call-done, f32[256,8192]{1,0:T(8,128)S(1)} %get-tuple-element.33, f32[256]{0:T(256)S(1)} %broadcast_maximum_fusion, s32[256]{0:T(256)S(1)} %le.48, s32[8192]{0:T(1024)S(1)} %convert_reduce_fusion.1, s32[256]{0:T(256)S(1)} %eq.54, f32[256]{0:T(256)S(1)} %fusion.9), kind=kOutput, calls=%fused_computation.49 | convolution fusion | flops 2160197632 | bytes 17338368 | tf_op jit(solution)/shard_map/dot_general | solution.py:97
  119.5 0.3 reshape.240
  119.8 0.5 convolution_convert_fusion.5
  120.3 0.3 convolution_convert_fusion.3
  120.6 0.8 copy.143
  121.5 4.0 all-to-all-start
  125.5 0.7 fusion.18
  126.2 8.2 %all-to-all-done = bf16[4,128,512]{2,1,0:T(8,128)(2,1)S(1)} async-done(((bf16[4,128,512]{2,1,0:T(8,128)(2,1)}), bf16[4,128,512]{2,1,0:T(8,128)(2,1)S(1)}, u32[]{:S(2)}, u32[]{:S(2)}) %all-to-all-start) | async-done | bytes 524320 | tf_op jit(solution)/shard_map/all_to_all | solution.py:116
  134.5 0.6 convolution_convert_fusion.2
  135.2 0.5 fusion.92
  135.7 39.2 %all_to_all.30 = bf16[64,12,512]{2,1,0:T(8,128)(2,1)S(1)} all-to-all(bf16[64,12,512]{2,1,0:T(8,128)(2,1)S(1)} %get-tuple-element.8), channel_id=1, replica_groups=mesh['seq'=64,'tp'=4] {'seq'}, dimensions={0} | all-to-all | bytes 1572864 | tf_op jit(solution)/shard_map/all_to_all | solution.py:145
  174.9 1.1 reshape.245
  176.0 34.5 %all_to_all.31 = bf16[64,12,512]{2,1,0:T(8,128)(2,1)S(1)} all-to-all(bf16[64,12,512]{2,1,0:T(8,128)(2,1)S(1)} %get-tuple-element.9), channel_id=1, replica_groups=mesh['seq'=64,'tp'=4] {'seq'}, dimensions={0} | all-to-all | bytes 1572864 | tf_op jit(solution)/shard_map/all_to_all | solution.py:145
  210.6 1.1 reshape.247
  211.8 1.2 all-gather.6.cloned.1.call-done
  213.0 2.7 fusion.3
  215.8 3.8 fusion.27
  219.6 7.6 %convolution_convert_fusion.1 = bf16[768,2048]{1,0:T(8,128)(2,1)} fusion(bf16[1,352,2048]{2,1,0:T(8,128)(2,1)} %param.25, bf16[1,2048,352]{1,2,0:T(8,128)(2,1)} %param.24, f32[768,352]{0,1:T(8,128)} %fusion.27, bf16[768,2048]{1,0:T(8,128)(2,1)S(1)} %copy-done.4, f32[2048]{0:T(1024)S(1)} %copy-done.12, f32[768]{0:T(1024)S(1)} %add_rsqrt_fusion.1), kind=kOutput, calls=%fused_computation.27 | convolution fusion | flops 2224078848 | bytes 10267648 | tf_op jit(solution)/shard_map/dot_general | solution.py:157
  227.5 29.6 %all-gather.8.cloned.1.call-done = bf16[768,2048]{1,0:T(8,128)(2,1)} async-done(((bf16[768,512]{1,0:T(8,128)(2,1)}), bf16[768,2048]{1,0:T(8,128)(2,1)}) %all-gather.8.cloned.1.call-update) | async-done | bytes 3145744 | tf_op jit(solution)/shard_map/all_gather | solution.py:148
  257.1 2.7 fusion.6
  259.9 3.8 fusion.25
  263.7 7.6 %convolution_convert_fusion = bf16[768,2048]{1,0:T(8,128)(2,1)} fusion(bf16[1,352,2048]{2,1,0:T(8,128)(2,1)} %param.25, bf16[1,2048,352]{1,2,0:T(8,128)(2,1)} %param.24, f32[768,352]{0,1:T(8,128)} %fusion.25, bf16[768,2048]{1,0:T(8,128)(2,1)S(1)} %copy-done.3, f32[768]{0:T(1024)S(1)} %add_rsqrt_fusion, f32[2048]{0:T(1024)S(1)} %copy-done.12), kind=kOutput, calls=%fused_computation.26 | convolution fusion | flops 2224078848 | bytes 10267648 | tf_op jit(solution)/shard_map/dot_general | solution.py:157
  271.3 29.3 %reduce-scatter.3.cloned.1.call-done = bf16[768,512]{1,0:T(8,128)(2,1)} async-done(((bf16[768,2048]{1,0:T(8,128)(2,1)}), bf16[768,512]{1,0:T(8,128)(2,1)}) %reduce-scatter.3.cloned.1.call-update) | async-done | bytes 786448 | tf_op jit(solution)/shard_map/reduce_scatter | solution.py:160
  300.6 2.1 reshape.246
  302.8 10.9 %all-to-all-start.2 = ((bf16[64,12,512]{2,1,0:T(8,128)(2,1)}), bf16[64,12,512]{2,1,0:T(8,128)(2,1)S(1)}, u32[]{:S(2)}, u32[]{:S(2)}) async-start(bf16[64,12,512]{2,1,0:T(8,128)(2,1)} %reshape.246), calls=%async_computation.3 | async-start | bytes 2097152 | tf_op jit(solution)/shard_map/all_to_all | solution.py:163
  313.6 30.0 %reduce-scatter.5.cloned.1.call-done = bf16[768,512]{1,0:T(8,128)(2,1)} async-done(((bf16[768,2048]{1,0:T(8,128)(2,1)}), bf16[768,512]{1,0:T(8,128)(2,1)}) %reduce-scatter.5.cloned.1.call-update) | async-done | bytes 786448 | tf_op jit(solution)/shard_map/reduce_scatter | solution.py:160
  343.7 2.2 reshape.248
  345.8 10.9 %all-to-all-start.4 = ((bf16[64,12,512]{2,1,0:T(8,128)(2,1)}), bf16[64,12,512]{2,1,0:T(8,128)(2,1)}, u32[]{:S(2)}, u32[]{:S(2)}) async-start(bf16[64,12,512]{2,1,0:T(8,128)(2,1)} %reshape.248), calls=%async_computation.6 | async-start | bytes 2097152 | tf_op jit(solution)/shard_map/all_to_all | solution.py:163
  357.0 28.2 %all-to-all-done.4 = bf16[64,12,512]{2,1,0:T(8,128)(2,1)} async-done(((bf16[64,12,512]{2,1,0:T(8,128)(2,1)}), bf16[64,12,512]{2,1,0:T(8,128)(2,1)}, u32[]{:S(2)}, u32[]{:S(2)}) %all-to-all-start.4) | async-done | bytes 786464 | tf_op jit(solution)/shard_map/all_to_all | solution.py:163
  385.2 1.7 pad_maximum_fusion
  386.9 2.7 gather_fusion
  389.9 1.1 fusion.93
  391.0 1.1 fusion.67
  392.2 11.7 %all_to_all.32 = bf16[4,128,512]{2,1,0:T(8,128)(2,1)S(1)} all-to-all(bf16[4,128,512]{2,1,0:T(8,128)(2,1)S(1)} %broadcast_in_dim.20), channel_id=1, replica_groups=mesh['seq'=64,'tp'=4] {'tp'}, dimensions={0} | all-to-all | bytes 1048576 | tf_op jit(solution)/shard_map/all_to_all | solution.py:176
  403.9 0.3 copy.111
  404.2 1.0 copy.112
  (74 shorter events, 3.8 us)
Async XLA Ops:
  7.2 1.9 copy-start
  7.2 5.2 %copy-start.2 = (bf16[128,2048]{1,0:T(8,128)(2,1)S(1)}, bf16[128,2048]{1,0:T(8,128)(2,1)}, u32[]{:S(2)}) copy-start(bf16[128,2048]{1,0:T(8,128)(2,1)} %param.13) | copy-start | bytes 1572868
  7.2 4.0 copy-start.11
  7.2 4.8 %copy-start.9 = (s32[128,6]{0,1:T(8,128)S(1)}, s32[128,6]{0,1:T(8,128)}, u32[]{:S(2)}) copy-start(s32[128,6]{0,1:T(8,128)} %param.21) | copy-start | bytes 9220
  7.2 96.3 %all-gather.4.cloned.1.call-start = ((), (), s32[]{:S(2)}) async-start(), calls=%async_computation.8 | async-start | bytes 9584640 | tf_op jit(solution)/shard_map/all_gather | solution.py:84
  9.0 6.1 %copy-start.8 = (bf16[2,512,256]{2,1,0:T(8,128)(2,1)S(1)}, bf16[2,512,256]{2,1,0:T(8,128)(2,1)}, u32[]{:S(2)}) copy-start(bf16[2,512,256]{2,1,0:T(8,128)(2,1)} %param.18) | copy-start | bytes 1572868
  113.1 7.2 %copy-start.7 = (bf16[256,2048]{1,0:T(8,128)(2,1)S(1)}, bf16[256,2048]{1,0:T(8,128)(2,1)}, u32[]{:S(2)}) copy-start(bf16[256,2048]{1,0:T(8,128)(2,1)} %param.19) | copy-start | bytes 3145732
  121.5 13.0 %all-to-all-start = ((bf16[4,128,512]{2,1,0:T(8,128)(2,1)}), bf16[4,128,512]{2,1,0:T(8,128)(2,1)S(1)}, u32[]{:S(2)}, u32[]{:S(2)}) async-start(bf16[4,128,512]{2,1,0:T(8,128)(2,1)} %bitcast.120), calls=%async_computation | async-start | bytes 1048576 | tf_op jit(solution)/shard_map/all_to_all | solution.py:116
  125.4 87.6 %all-gather.6.cloned.1.call-start = ((), (), s32[]{:S(2)}) async-start(), calls=%async_computation.9 | async-start | bytes 3932160 | tf_op jit(solution)/shard_map/all_gather | solution.py:148
  134.5 0.7 copy-start.5
  176.0 81.1 %all-gather.8.cloned.1.call-start = ((), (), s32[]{:S(2)}) async-start(), calls=%async_computation.11 | async-start | bytes 3932160 | tf_op jit(solution)/shard_map/all_gather | solution.py:148
  210.6 5.2 %copy-start.12 = (f32[2048]{0:T(1024)S(1)}, f32[2048]{0:T(1024)}, u32[]{:S(2)}) copy-start(f32[2048]{0:T(1024)} %param.20) | copy-start | bytes 24580
  211.7 88.9 %reduce-scatter.3.cloned.1.call-start = ((), (), s32[]{:S(2)}) async-start(), calls=%async_computation.10 | async-start | bytes 3932160 | tf_op jit(solution)/shard_map/reduce_scatter | solution.py:160
  213.0 2.8 copy-start.4
  227.2 116.4 %reduce-scatter.5.cloned.1.call-start = ((), (), s32[]{:S(2)}) async-start(), calls=%async_computation.12 | async-start | bytes 3932160 | tf_op jit(solution)/shard_map/reduce_scatter | solution.py:160
  257.1 2.8 copy-start.3
  302.8 54.2 %copy-start.10 = (f32[128,6]{0,1:T(8,128)S(1)}, f32[128,6]{0,1:T(8,128)}, u32[]{:S(2)}) copy-start(f32[128,6]{0,1:T(8,128)} %param.22) | copy-start | bytes 9220
  302.8 43.1 %all-to-all-start.2 = ((bf16[64,12,512]{2,1,0:T(8,128)(2,1)}), bf16[64,12,512]{2,1,0:T(8,128)(2,1)S(1)}, u32[]{:S(2)}, u32[]{:S(2)}) async-start(bf16[64,12,512]{2,1,0:T(8,128)(2,1)} %reshape.246), calls=%async_computation.3 | async-start | bytes 2097152 | tf_op jit(solution)/shard_map/all_to_all | solution.py:163
  345.8 39.4 %all-to-all-start.4 = ((bf16[64,12,512]{2,1,0:T(8,128)(2,1)}), bf16[64,12,512]{2,1,0:T(8,128)(2,1)}, u32[]{:S(2)}, u32[]{:S(2)}) async-start(bf16[64,12,512]{2,1,0:T(8,128)(2,1)} %reshape.248), calls=%async_computation.6 | async-start | bytes 2097152 | tf_op jit(solution)/shard_map/all_to_all | solution.py:163
  389.9 1.2 copy-start.6
  389.9 15.3 %copy-start.1 = (bf16[2048,576]{0,1:T(8,128)(2,1)S(1)}, bf16[2048,576]{0,1:T(8,128)(2,1)}, u32[]{:S(2)}) copy-start(bf16[2048,576]{0,1:T(8,128)(2,1)} %param.16) | copy-start | bytes 7077892
Sparse Core Ops, SparseCore 0:
  12.1 91.3 all-gather.3
  176.1 36.8 all-gather.5
  214.8 42.2 all-gather.7
  259.5 41.1 reduce-scatter.2
  303.0 40.5 reduce-scatter.4
where the time goes:
time: 412 us
  waiting for transfers between devices  211 us (51%)
  blocking collectives  85.4 us (21%)
  matrix products  41.3 us (10%)
  starting transfers between devices  26.2 us (6%)
  other arithmetic  18 us (4%)
  local copies, waits for them, and re-layouts  15.3 us (4%)
  between operations  14.2 us (3%)
    all_gather x1, waiting for transfers between devices, on_device(): shard_rows = lax.all_gather(latent, 'seq', axis=0, tiled=True)  84.7 us
    all_to_all x2, blocking collectives, on_device(): lax.all_to_all(sending, 'seq', split_axis=0, concat_axis=0, tiled=True)  73.7 us
    reduce_scatter x2, waiting for transfers between devices, on_device(): lax.psum_scatter(expert_out, 'tp', scatter_dimension=1, tiled=True)  59.3 us
    all_gather x2, waiting for transfers between devices, on_device(): lax.all_gather(flat_part, 'tp', axis=1, tiled=True).astype(jnp.float32)  30.8 us
    all_to_all x2, waiting for transfers between devices, on_device(): lax.all_to_all(expert_sum, 'seq', split_axis=0, concat_axis=0, tiled=True)  28.2 us
    all_to_all x2, starting transfers between devices, on_device(): lax.all_to_all(expert_sum, 'seq', split_axis=0, concat_axis=0, tiled=True)  21.8 us
    dot_general x2, matrix products, on_device(): jnp.dot(hidden_units, expert_down[0], preferred_element_type=jnp.float32)  15.2 us
    all_to_all x1, blocking collectives, on_device(): lax.all_to_all(repeated_part, 'tp', split_axis=0, concat_axis=0, tiled=True)  11.7 us
  transfers between devices with their start and end apart: 8, of which 7 were waited for; matrix products, arithmetic and copies ran while one was open for 10% of the time, Pallas kernels for 0%

commit v1 on v0

--- a/solution.py
+++ b/solution.py
@@ -81,7 +81,9 @@
     row_segment = jnp.repeat(segment, head_count)
     row_index = jnp.repeat(token_index, head_count)
     row_total = tok_count * head_count
-    shard_rows = lax.all_gather(latent, "seq", axis=0, tiled=True)
+    shard_rows = jnp.concatenate(
+        lax.all_to_all(jnp.stack([latent] * lax.axis_size("seq")), "seq", 0, 0), axis=0
+    )
     key_count = shard_rows.shape[0]
     key_index = jnp.arange(key_count, dtype=jnp.int32)
     key_segment, unused = place(key_index, lengths)

time: 412 us -> 558 us (1.35)
  waiting for transfers between devices: 211 us -> 330 us
  local copies, waits for them, and re-layouts: 15.3 us -> 33.1 us
  starting transfers between devices: 26.2 us -> 39.7 us
    all_to_all x0 -> x1, waiting for transfers between devices: none -> 203 us  [on_device(): lax.all_to_all(jnp.stack([latent] * lax.axis_size('seq')), 'seq', 0, 0)]
    all_gather x1 -> x0, waiting for transfers between devices: 84.7 us -> none  [on_device(): shard_rows = lax.all_gather(latent, 'seq', axis=0, tiled=True)]
    all_to_all x0 -> x1, starting transfers between devices: none -> 13.5 us  [on_device(): lax.all_to_all(jnp.stack([latent] * lax.axis_size('seq')), 'seq', 0, 0)]
    reshape x0 -> x1, local copies, waits for them, and re-layouts: none -> 8.73 us  [on_device(): jnp.concatenate(lax.all_to_all(jnp.stack([latent] * lax.axis_size('seq'))...]
    another operation x0 -> x1, local copies, waits for them, and re-layouts: none -> 5.93 us  [on_device(): jnp.stack([latent] * lax.axis_size('seq'))]
  transfers between devices with their start and end apart: 8 -> 8, of which waited for: 7 -> 7; matrix products, arithmetic and copies ran while one was open for 10% -> 7% of each run, Pallas kernels for 0% -> 0%
where the time goes in v1:
time: 558 us; the launch traced here: 557 us
  waiting for transfers between devices  330 us (59%)
  blocking collectives  80.1 us (14%)
  matrix products  42 us (8%)
  starting transfers between devices  39.7 us (7%)
  local copies, waits for them, and re-layouts  33.1 us (6%)
  other arithmetic  17.3 us (3%)
  between operations  14.3 us (3%)
    all_to_all x1, waiting for transfers between devices, on_device(): lax.all_to_all(jnp.stack([latent] * lax.axis_size('seq')), 'seq', 0, 0)  203 us
    all_to_all x2, blocking collectives, on_device(): lax.all_to_all(sending, 'seq', split_axis=0, concat_axis=0, tiled=True)  68.4 us
    reduce_scatter x2, waiting for transfers between devices, on_device(): lax.psum_scatter(expert_out, 'tp', scatter_dimension=1, tiled=True)  59.9 us
    all_gather x2, waiting for transfers between devices, on_device(): lax.all_gather(flat_part, 'tp', axis=1, tiled=True).astype(jnp.float32)  30.2 us
    all_to_all x2, waiting for transfers between devices, on_device(): lax.all_to_all(expert_sum, 'seq', split_axis=0, concat_axis=0, tiled=True)  28.2 us
    all_to_all x2, starting transfers between devices, on_device(): lax.all_to_all(expert_sum, 'seq', split_axis=0, concat_axis=0, tiled=True)  21.8 us
    dot_general x2, matrix products, on_device(): jnp.dot(hidden_units, expert_down[0], preferred_element_type=jnp.float32)  16.7 us
    all_to_all x1, starting transfers between devices, on_device(): lax.all_to_all(jnp.stack([latent] * lax.axis_size('seq')), 'seq', 0, 0)  13.5 us
  transfers between devices with their start and end apart: 8, of which 7 were waited for; matrix products, arithmetic and copies ran while one was open for 7% of the time, Pallas kernels for 0%

profile of v1, /device:TPU:1, one launch (start us, length us, event | category | flops | bytes accessed | tf_op | source)
XLA Modules:
  0.0 556.8 jit_solution(14363406447608806796)
XLA Ops:
  7.2 1.0 reduce-window.18
  8.2 0.7 fusion.82
  9.0 1.8 fusion.94
  11.2 5.9 %stack.2 = bf16[64,128,576]{1,2,0:T(8,128)(2,1)} broadcast(bf16[128,576]{0,1:T(8,128)(2,1)S(1)} %pad_maximum_fusion.1), dimensions={1,2} | broadcast | bytes 9584640 | tf_op jit(solution)/shard_map/stack | solution.py:85
  17.2 13.5 %all-to-all-start = ((bf16[64,128,576]{1,2,0:T(8,128)(2,1)}), bf16[64,128,576]{1,2,0:T(8,128)(2,1)}, u32[]{:S(2)}, u32[]{:S(2)}) async-start(bf16[64,128,576]{1,2,0:T(8,128)(2,1)} %stack.2), calls=%async_computation | async-start | bytes 18874368 | tf_op jit(solution)/shard_map/all_to_all | solution.py:85
  31.1 0.4 convolution_convert_fusion.4
  32.6 0.4 copy.99
  33.1 0.4 concatenate.19
  33.5 1.8 reduce-window.19
  36.0 202.9 %all-to-all-done = bf16[64,128,576]{1,2,0:T(8,128)(2,1)} async-done(((bf16[64,128,576]{1,2,0:T(8,128)(2,1)}), bf16[64,128,576]{1,2,0:T(8,128)(2,1)}, u32[]{:S(2)}, u32[]{:S(2)}) %all-to-all-start) | async-done | bytes 9437216 | tf_op jit(solution)/shard_map/all_to_all | solution.py:85
  238.9 6.7 %select_reduce_fusion = (f32[256]{0:T(256)S(1)}, f32[256,8192]{1,0:T(8,128)S(1)}) fusion(s32[256]{0:T(256)S(1)} %le.48, s32[8192]{0:T(1024)S(1)} %convert_reduce_fusion.1, s32[256]{0:T(256)S(1)} %eq.54, f32[256,32]{1,0:T(8,128)S(1)} %bitcast.140, f32[256,32]{1,0:T(8,128)S(1)} %bitcast.139, f32[256,512]{1,0:T(8,128)S(1)} %concatenate.19, ...), kind=kOutput, calls=%fused_computation.5 | convolution fusion | flops 2426994432 | bytes 18451456 | tf_op jit(solution)/shard_map/ra,ka->rk/dot_general | solution.py:94
  245.6 3.3 copy-done.2
  248.9 2.7 fusion.9
  251.7 8.7 %copy_bitcast_fusion = bf16[8192,576]{0,1:T(8,128)(2,1)} fusion(bf16[64,128,576]{1,2,0:T(8,128)(2,1)} %all-to-all-done), kind=kLoop, calls=%fused_computation.1 | loop fusion | bytes 18874368 | tf_op jit(solution)/shard_map/reshape | solution.py:84
  260.4 8.4 %fusion.41 = f32[256,512]{1,0:T(8,128)S(1)} fusion(bf16[8192,576]{0,1:T(8,128)(2,1)} %copy_bitcast_fusion, f32[256,8192]{1,0:T(8,128)} %copy-done.2, f32[256]{0:T(256)S(1)} %broadcast_maximum_fusion, s32[256]{0:T(256)S(1)} %le.48, s32[8192]{0:T(1024)S(1)} %convert_reduce_fusion.1, s32[256]{0:T(256)S(1)} %eq.54, f32[256]{0:T(256)S(1)} %fusion.9), kind=kOutput, calls=%fused_computation.50 | convolution fusion | flops 2160197632 | bytes 17338368 | tf_op jit(solution)/shard_map/dot_general | solution.py:99
  269.1 0.5 convolution_convert_fusion.5
  269.6 0.3 convolution_convert_fusion.3
  269.9 0.8 copy.153
  270.8 4.0 all-to-all-start.1
  274.9 0.7 fusion.18
  275.6 9.1 %all-to-all-done.1 = bf16[4,128,512]{2,1,0:T(8,128)(2,1)S(1)} async-done(((bf16[4,128,512]{2,1,0:T(8,128)(2,1)}), bf16[4,128,512]{2,1,0:T(8,128)(2,1)S(1)}, u32[]{:S(2)}, u32[]{:S(2)}) %all-to-all-start.1) | async-done | bytes 524320 | tf_op jit(solution)/shard_map/all_to_all | solution.py:118
  284.8 0.6 convolution_convert_fusion.2
  285.4 0.5 fusion.92
  285.8 33.9 %all_to_all.35 = bf16[64,12,512]{2,1,0:T(8,128)(2,1)S(1)} all-to-all(bf16[64,12,512]{2,1,0:T(8,128)(2,1)S(1)} %get-tuple-element.8), channel_id=1, replica_groups=mesh['seq'=64,'tp'=4] {'seq'}, dimensions={0} | all-to-all | bytes 1572864 | tf_op jit(solution)/shard_map/all_to_all | solution.py:147
  319.8 1.1 reshape.259
  320.9 34.5 %all_to_all.36 = bf16[64,12,512]{2,1,0:T(8,128)(2,1)S(1)} all-to-all(bf16[64,12,512]{2,1,0:T(8,128)(2,1)S(1)} %get-tuple-element.9), channel_id=1, replica_groups=mesh['seq'=64,'tp'=4] {'seq'}, dimensions={0} | all-to-all | bytes 1572864 | tf_op jit(solution)/shard_map/all_to_all | solution.py:147
  355.4 1.0 reshape.261
  356.5 1.3 all-gather.3.cloned.1.call-done
  357.8 2.7 fusion.3
  360.7 3.9 fusion.27
  364.6 8.1 %convolution_convert_fusion.1 = bf16[768,2048]{1,0:T(8,128)(2,1)} fusion(bf16[1,352,2048]{2,1,0:T(8,128)(2,1)S(1)} %copy-done.16, bf16[1,2048,352]{1,2,0:T(8,128)(2,1)} %param.24, f32[768,352]{0,1:T(8,128)} %fusion.27, bf16[768,2048]{1,0:T(8,128)(2,1)} %all-gather.3.cloned.1.call-done, f32[2048]{0:T(1024)S(1)} %copy-done.17, f32[768]{0:T(1024)S(1)} %add_rsqrt_fusion.1), kind=kOutput, calls=%fused_computation.28 | convolution fusion | flops 2224078848 | bytes 10267648 | tf_op jit(solution)/shard_map/dot_general | solution.py:159
  373.0 28.9 %all-gather.5.cloned.1.call-done = bf16[768,2048]{1,0:T(8,128)(2,1)} async-done(((bf16[768,512]{1,0:T(8,128)(2,1)}), bf16[768,2048]{1,0:T(8,128)(2,1)}) %all-gather.5.cloned.1.call-update) | async-done | bytes 3145744 | tf_op jit(solution)/shard_map/all_gather | solution.py:150
  401.9 2.7 fusion.6
  404.7 2.4 fusion.25
  407.1 8.6 %convolution_convert_fusion = bf16[768,2048]{1,0:T(8,128)(2,1)} fusion(bf16[1,352,2048]{2,1,0:T(8,128)(2,1)} %param.25, bf16[1,2048,352]{1,2,0:T(8,128)(2,1)} %param.24, f32[768,352]{0,1:T(8,128)} %fusion.25, bf16[768,2048]{1,0:T(8,128)(2,1)} %all-gather.5.cloned.1.call-done, f32[768]{0:T(1024)S(1)} %add_rsqrt_fusion, f32[2048]{0:T(1024)S(1)} %copy-done.17), kind=kOutput, calls=%fused_computation.27 | convolution fusion | flops 2224078848 | bytes 10267648 | tf_op jit(solution)/shard_map/dot_general | solution.py:159
  415.7 29.9 %reduce-scatter.3.cloned.1.call-done = bf16[768,512]{1,0:T(8,128)(2,1)} async-done(((bf16[768,2048]{1,0:T(8,128)(2,1)}), bf16[768,512]{1,0:T(8,128)(2,1)}) %reduce-scatter.3.cloned.1.call-update) | async-done | bytes 786448 | tf_op jit(solution)/shard_map/reduce_scatter | solution.py:162
  445.6 2.1 reshape.260
  447.8 10.9 %all-to-all-start.3 = ((bf16[64,12,512]{2,1,0:T(8,128)(2,1)}), bf16[64,12,512]{2,1,0:T(8,128)(2,1)S(1)}, u32[]{:S(2)}, u32[]{:S(2)}) async-start(bf16[64,12,512]{2,1,0:T(8,128)(2,1)} %reshape.260), calls=%async_computation.4 | async-start | bytes 2097152 | tf_op jit(solution)/shard_map/all_to_all | solution.py:165
  458.6 30.0 %reduce-scatter.5.cloned.1.call-done = bf16[768,512]{1,0:T(8,128)(2,1)} async-done(((bf16[768,2048]{1,0:T(8,128)(2,1)}), bf16[768,512]{1,0:T(8,128)(2,1)}) %reduce-scatter.5.cloned.1.call-update) | async-done | bytes 786448 | tf_op jit(solution)/shard_map/reduce_scatter | solution.py:162
  488.7 2.2 reshape.262
  490.8 10.9 %all-to-all-start.5 = ((bf16[64,12,512]{2,1,0:T(8,128)(2,1)}), bf16[64,12,512]{2,1,0:T(8,128)(2,1)}, u32[]{:S(2)}, u32[]{:S(2)}) async-start(bf16[64,12,512]{2,1,0:T(8,128)(2,1)} %reshape.262), calls=%async_computation.7 | async-start | bytes 2097152 | tf_op jit(solution)/shard_map/all_to_all | solution.py:165
  502.0 28.2 %all-to-all-done.5 = bf16[64,12,512]{2,1,0:T(8,128)(2,1)} async-done(((bf16[64,12,512]{2,1,0:T(8,128)(2,1)}), bf16[64,12,512]{2,1,0:T(8,128)(2,1)}, u32[]{:S(2)}, u32[]{:S(2)}) %all-to-all-start.5) | async-done | bytes 786464 | tf_op jit(solution)/shard_map/all_to_all | solution.py:165
  530.2 1.7 pad_maximum_fusion
  531.9 2.7 gather_fusion
  534.9 1.1 fusion.93
  536.0 1.1 fusion.67
  537.2 11.7 %all_to_all.37 = bf16[4,128,512]{2,1,0:T(8,128)(2,1)S(1)} all-to-all(bf16[4,128,512]{2,1,0:T(8,128)(2,1)S(1)} %broadcast_in_dim.20), channel_id=1, replica_groups=mesh['seq'=64,'tp'=4] {'tp'}, dimensions={0} | all-to-all | bytes 1048576 | tf_op jit(solution)/shard_map/all_to_all | solution.py:178
  549.2 1.0 copy.117
  (85 shorter events, 4.5 us)
Async XLA Ops:
  7.2 1.8 copy-start
  7.2 3.9 copy-start.14
  11.2 5.9 %copy-start.10 = (bf16[128,576]{0,1:T(8,128)(2,1)}, bf16[128,576]{0,1:T(8,128)(2,1)S(1)}, u32[]{:S(2)}) copy-start(bf16[128,576]{0,1:T(8,128)(2,1)S(1)} %pad_maximum_fusion.1) | copy-start | bytes 442372
  17.2 13.5 %copy-start.12 = (s32[128,6]{0,1:T(8,128)S(1)}, s32[128,6]{0,1:T(8,128)}, u32[]{:S(2)}) copy-start(s32[128,6]{0,1:T(8,128)} %param.21) | copy-start | bytes 9220
  17.2 13.9 %copy-start.3 = (bf16[128,2048]{1,0:T(8,128)(2,1)S(1)}, bf16[128,2048]{1,0:T(8,128)(2,1)}, u32[]{:S(2)}) copy-start(bf16[128,2048]{1,0:T(8,128)(2,1)} %param.13) | copy-start | bytes 1572868
  17.2 13.9 %copy-start.8 = (bf16[2048,384]{1,0:T(8,128)(2,1)S(1)}, bf16[2048,384]{1,0:T(8,128)(2,1)}, u32[]{:S(2)}) copy-start(bf16[2048,384]{1,0:T(8,128)(2,1)} %param.15) | copy-start | bytes 4718596
  17.2 221.7 %all-to-all-start = ((bf16[64,128,576]{1,2,0:T(8,128)(2,1)}), bf16[64,128,576]{1,2,0:T(8,128)(2,1)}, u32[]{:S(2)}, u32[]{:S(2)}) async-start(bf16[64,128,576]{1,2,0:T(8,128)(2,1)} %stack.2), calls=%async_computation | async-start | bytes 18874368 | tf_op jit(solution)/shard_map/all_to_all | solution.py:85
  30.6 1.7 copy-start.11
  245.6 3.4 copy-start.2
  260.4 9.2 %copy-start.9 = (bf16[256,2048]{1,0:T(8,128)(2,1)S(1)}, bf16[256,2048]{1,0:T(8,128)(2,1)}, u32[]{:S(2)}) copy-start(bf16[256,2048]{1,0:T(8,128)(2,1)} %param.19) | copy-start | bytes 3145732
  270.8 13.9 %all-to-all-start.1 = ((bf16[4,128,512]{2,1,0:T(8,128)(2,1)}), bf16[4,128,512]{2,1,0:T(8,128)(2,1)S(1)}, u32[]{:S(2)}, u32[]{:S(2)}) async-start(bf16[4,128,512]{2,1,0:T(8,128)(2,1)} %bitcast.130), calls=%async_computation.1 | async-start | bytes 1048576 | tf_op jit(solution)/shard_map/all_to_all | solution.py:118
  274.8 83.0 %all-gather.3.cloned.1.call-start = ((), (), s32[]{:S(2)}) async-start(), calls=%async_computation.9 | async-start | bytes 3932160 | tf_op jit(solution)/shard_map/all_gather | solution.py:150
  284.8 1.1 copy-start.6
  320.8 81.1 %all-gather.5.cloned.1.call-start = ((), (), s32[]{:S(2)}) async-start(), calls=%async_computation.11 | async-start | bytes 3932160 | tf_op jit(solution)/shard_map/all_gather | solution.py:150
  355.4 5.2 copy-start.17
  356.5 89.2 %reduce-scatter.3.cloned.1.call-start = ((), (), s32[]{:S(2)}) async-start(), calls=%async_computation.10 | async-start | bytes 3932160 | tf_op jit(solution)/shard_map/reduce_scatter | solution.py:162
  357.8 2.8 copy-start.5
  360.7 3.9 copy-start.16
  372.7 32.0 %copy-start.15 = (bf16[1,2048,352]{1,2,0:T(8,128)(2,1)S(1)}, bf16[1,2048,352]{1,2,0:T(8,128)(2,1)}, u32[]{:S(2)}) copy-start(bf16[1,2048,352]{1,2,0:T(8,128)(2,1)} %param.23) | copy-start | bytes 4325380
  372.7 115.9 %reduce-scatter.5.cloned.1.call-start = ((), (), s32[]{:S(2)}) async-start(), calls=%async_computation.12 | async-start | bytes 3932160 | tf_op jit(solution)/shard_map/reduce_scatter | solution.py:162
  401.9 2.8 copy-start.4
  447.8 54.2 %copy-start.13 = (f32[128,6]{0,1:T(8,128)S(1)}, f32[128,6]{0,1:T(8,128)}, u32[]{:S(2)}) copy-start(f32[128,6]{0,1:T(8,128)} %param.22) | copy-start | bytes 9220
  447.8 43.1 %all-to-all-start.3 = ((bf16[64,12,512]{2,1,0:T(8,128)(2,1)}), bf16[64,12,512]{2,1,0:T(8,128)(2,1)S(1)}, u32[]{:S(2)}, u32[]{:S(2)}) async-start(bf16[64,12,512]{2,1,0:T(8,128)(2,1)} %reshape.260), calls=%async_computation.4 | async-start | bytes 2097152 | tf_op jit(solution)/shard_map/all_to_all | solution.py:165
  490.8 39.4 %all-to-all-start.5 = ((bf16[64,12,512]{2,1,0:T(8,128)(2,1)}), bf16[64,12,512]{2,1,0:T(8,128)(2,1)}, u32[]{:S(2)}, u32[]{:S(2)}) async-start(bf16[64,12,512]{2,1,0:T(8,128)(2,1)} %reshape.262), calls=%async_computation.7 | async-start | bytes 2097152 | tf_op jit(solution)/shard_map/all_to_all | solution.py:165
  534.9 1.2 copy-start.7
  534.9 15.3 %copy-start.1 = (bf16[2048,576]{0,1:T(8,128)(2,1)S(1)}, bf16[2048,576]{0,1:T(8,128)(2,1)}, u32[]{:S(2)}) copy-start(bf16[2048,576]{0,1:T(8,128)(2,1)} %param.16) | copy-start | bytes 7077892
Sparse Core Ops, SparseCore 0:
  321.0 36.8 all-gather.2
  359.6 42.2 all-gather.4
  404.5 41.1 reduce-scatter.2
  448.0 40.5 reduce-scatter.4
